TPU v7x, 32 devices: a whole 2x2x4 slice. The times are simulated.
32 devices in a mesh: groups: 2 (over y), blk: 4 (over z), head: 2 (over x), rep: 2 (over core).
Axes of the slice: x: 2, y: 2, z: 4, core: 2. Of those that a mesh axis runs over, the one named last changes fastest.
Arguments:
- queries: bfloat16 [4, 4096, 1024], P('groups', ('blk', 'rep'), 'head'), parts along dimension 0, may hold values from -24 to 24
- prefix_keys: bfloat16 [4, 8192, 128], P('groups', ('blk', 'head')), parts along dimension 0, may hold values from -6 to 6
- prefix_values: bfloat16 [4, 8192, 128], P('groups', ('blk', 'head')), parts along dimension 0, may hold values from -6 to 6
- stretch_keys: bfloat16 [4, 4096, 128], P('groups', ('blk', 'head')), parts along dimension 0, may hold values from -6 to 6
- stretch_values: bfloat16 [4, 4096, 128], P('groups', ('blk', 'head')), parts along dimension 0, may hold values from -6 to 6
- prefix_lengths: int32 [4], P('groups'), parts along dimension 0, may hold values from 128 to 8192, as said below
- decode_queries: bfloat16 [8, 64, 1024], P('groups', 'rep'), parts along dimension 0, may hold values from -24 to 24
- new_keys: bfloat16 [8, 64, 128], P('groups', 'rep'), parts along dimension 0, may hold values from -6 to 6
- new_values: bfloat16 [8, 64, 128], P('groups', 'rep'), parts along dimension 0, may hold values from -6 to 6
- row_prompts: int32 [128], P(('groups', 'rep')), parts along dimension 0, may hold values from 0 to 1
Outputs:
- prefill_out: bfloat16 [4, 4096, 1024], P('groups', ('blk', 'rep'), 'head'), parts along dimension 0
- decode_out: bfloat16 [8, 64, 1024], P('groups', 'rep'), parts along dimension 0
There are 2 independent parts, one for each index of `groups`. A program takes and returns all parts, laid end to end along the dimension named above; each array names one. Nothing has to cross between parts.
Inputs may be any that keep to these rules, and one draw needn't show every extreme that they name: `prefix_lengths`: multiples of 128; in every draw some prompt has exactly 8192.
All inputs are finite; a program needn't handle non-finite values.
Results may differ from a plain program's by a relative error of at most 0.0095.
Values may be sent and summed in bfloat16 or wider, within the bound.
A program may use at most 192 MiB of HBM per device.

v0:
```python
import jax
import jax.numpy as jnp
from jax import lax
from jax.sharding import PartitionSpec as P

HEAD_DIM = 128


def combined_all(value, axis, join):
    pieces = jax.tree.map(lambda part: lax.all_gather(part, axis), value)
    head = jax.tree.map(lambda part: part[0], pieces)
    tail = jax.tree.map(lambda part: part[1:], pieces)
    running, _ = lax.scan(lambda running, share: (join(running, share), None), head, tail)
    return running


def online_update(carried, scores, visible, values_block, einsum_form):
    running_max, totals, weighted = carried
    scores = jnp.where(visible, scores, -jnp.inf)
    updated = jnp.maximum(running_max, jnp.max(scores, axis=-1))
    anchor = jnp.where(jnp.isfinite(updated), updated, 0.0)
    weights = jnp.where(visible, jnp.exp(scores - anchor[..., None]), 0.0)
    factor = jnp.exp(running_max - anchor)
    totals = totals * factor + jnp.sum(weights, axis=-1)
    weighted = weighted * factor[..., None] + jnp.einsum(
        einsum_form, weights.astype(jnp.bfloat16), values_block, preferred_element_type=jnp.float32
    )
    return (updated, totals, weighted)


def merge_parts(former, latter):
    max_one, total_one, sum_one = former
    max_two, total_two, sum_two = latter
    updated = jnp.maximum(max_one, max_two)
    anchor = jnp.where(jnp.isfinite(updated), updated, 0.0)
    factor_one = jnp.exp(max_one - anchor)
    factor_two = jnp.exp(max_two - anchor)
    return (
        updated,
        total_one * factor_one + total_two * factor_two,
        sum_one * factor_one[..., None] + sum_two * factor_two[..., None],
    )


def make_fold(query_block, lengths, q_pos, q_start, pre_rows, chk_rows):
    scaling = HEAD_DIM ** (-0.5)
    prompts = query_block.shape[0]
    q_rows = query_block.shape[1]
    shard_len = pre_rows + chk_rows
    longest = jnp.max(lengths)

    def fold_rows(carried, pieces, root):
        piece_keys, piece_values = pieces
        blocks = piece_keys.shape[1] // shard_len
        grouped = 4
        span = grouped * shard_len
        turns = blocks // grouped
        keys_split = jnp.swapaxes(piece_keys.reshape(prompts, turns, span, HEAD_DIM), 0, 1)
        values_split = jnp.swapaxes(piece_values.reshape(prompts, turns, span, HEAD_DIM), 0, 1)
        first_shard = root // shard_len
        offsets = jnp.arange(span, dtype=jnp.int32)
        within = offsets % shard_len
        is_prefix = within < pre_rows

        def advance(carry_now, inputs):
            keys_now, values_now, turn_index = inputs
            shard_ids = turn_index * grouped + offsets // shard_len
            positions = jnp.where(
                is_prefix, shard_ids * pre_rows + within, shard_ids * chk_rows + within - pre_rows
            )
            prefix_ok = is_prefix[None, :] & (positions[None, :] < lengths[:, None])
            stretch_ok = (~is_prefix)[None, :] & (positions[None, :] <= q_pos[:, None])
            visible = prefix_ok[:, None, None, :] | stretch_ok[None, :, None, :]
            low_shard = turn_index * grouped

            def update(state_now):
                scores = (
                    jnp.einsum(
                        "pqhd,pkd->pqhk", query_block, keys_now, preferred_element_type=jnp.float32
                    )
                    * scaling
                )
                return online_update(state_now, scores, visible, values_now, "pqhk,pkd->pqhd")

            needed = (low_shard * pre_rows < longest) | (
                low_shard * chk_rows <= q_start + q_rows - 1
            )
            return (lax.cond(needed, update, lambda state_now: state_now, carry_now), None)

        carried, _ = lax.scan(
            advance, carried, (keys_split, values_split, jnp.arange(turns, dtype=jnp.int32))
        )
        return carried

    return fold_rows


def empty_state(prompts, q_rows, heads_count):
    return (
        jnp.full((prompts, q_rows, heads_count), -jnp.inf, jnp.float32),
        jnp.zeros((prompts, q_rows, heads_count), jnp.float32),
        jnp.zeros((prompts, q_rows, heads_count, HEAD_DIM), jnp.float32),
    )


def local(
    queries,
    prefix_keys,
    prefix_values,
    stretch_keys,
    stretch_values,
    prefix_lengths,
    decode_queries,
    new_keys,
    new_values,
    row_prompts,
):
    scaling = HEAD_DIM ** (-0.5)
    prompts, q_rows, width = queries.shape
    heads_dev = width // HEAD_DIM
    pre_rows = prefix_keys.shape[1]
    chk_rows = stretch_keys.shape[1]
    q_start = lax.axis_index(("blk", "rep")) * q_rows
    q_pos = q_start + jnp.arange(q_rows, dtype=jnp.int32)
    local_keys = jnp.concatenate([prefix_keys, stretch_keys], axis=1)
    local_values = jnp.concatenate([prefix_values, stretch_values], axis=1)
    all_prompts = jnp.arange(prompts, dtype=jnp.int32)
    regrouped = lax.all_to_all(queries, "head", split_axis=0, concat_axis=2, tiled=True)
    mine_count = regrouped.shape[0]
    mine_ids = lax.axis_index("head") * mine_count + jnp.arange(mine_count, dtype=jnp.int32)
    mine_lengths = jnp.sum(
        jnp.where(mine_ids[:, None] == all_prompts[None, :], prefix_lengths[None, :], 0), axis=1
    )
    query_block = regrouped.reshape(mine_count, q_rows, heads_dev * lax.axis_size("head"), HEAD_DIM)
    mine_keys, mine_values = (
        lax.all_to_all(local_keys, "head", split_axis=0, concat_axis=1, tiled=True),
        lax.all_to_all(local_values, "head", split_axis=0, concat_axis=1, tiled=True),
    )
    fold_rows = make_fold(query_block, mine_lengths, q_pos, q_start, pre_rows, chk_rows)
    initial = empty_state(mine_count, q_rows, query_block.shape[2])
    final_state = fold_rows(
        initial,
        (
            lax.all_gather(mine_keys, "blk", axis=1, tiled=True),
            lax.all_gather(mine_values, "blk", axis=1, tiled=True),
        ),
        jnp.int32(0),
    )
    mine_out = (
        (final_state[2] / final_state[1][..., None])
        .astype(jnp.bfloat16)
        .reshape(mine_count, q_rows, query_block.shape[2] * HEAD_DIM)
    )
    prefill_out = lax.all_to_all(mine_out, "head", split_axis=2, concat_axis=0, tiled=True)
    steps, row_dev, decode_width = decode_queries.shape
    heads_all = decode_width // HEAD_DIM
    relaid = (
        lax.all_to_all(prefix_keys, "head", split_axis=0, concat_axis=1, tiled=True),
        lax.all_to_all(prefix_values, "head", split_axis=0, concat_axis=1, tiled=True),
        lax.all_to_all(stretch_keys, "head", split_axis=0, concat_axis=1, tiled=True),
        lax.all_to_all(stretch_values, "head", split_axis=0, concat_axis=1, tiled=True),
    )
    cache_keys = jnp.concatenate([relaid[0], relaid[2]], axis=1)
    cache_values = jnp.concatenate([relaid[1], relaid[3]], axis=1)
    prompts_here = relaid[0].shape[0]
    prompt_ids = lax.axis_index("head") * prompts_here + jnp.arange(prompts_here, dtype=jnp.int32)
    pre_here = relaid[0].shape[1]
    pre_root = lax.axis_index("blk") * pre_here
    count_here, cache_len = (cache_keys.shape[0], cache_keys.shape[1])
    flat_keys = cache_keys.reshape(count_here * cache_len, HEAD_DIM)
    flat_values = cache_values.reshape(count_here * cache_len, HEAD_DIM)
    lengths_here = jnp.sum(
        jnp.where(prompt_ids[:, None] == all_prompts[None, :], prefix_lengths[None, :], 0), axis=1
    )
    cache_offsets = jnp.arange(cache_len, dtype=jnp.int32)
    key_live = (cache_offsets[None, :] >= pre_here) | (
        pre_root + cache_offsets[None, :] < lengths_here[:, None]
    )
    key_prompt = jnp.broadcast_to(prompt_ids[:, None], (count_here, cache_len)).reshape(-1)
    row_visible = (row_prompts[:, None] == key_prompt[None, :]) & key_live.reshape(-1)[None, :]
    all_visible = jnp.tile(row_visible, (steps, 1))[:, None, :]
    decode_rows = decode_queries.reshape(steps * row_dev, heads_all, HEAD_DIM)
    decode_scores = (
        jnp.einsum("rhd,kd->rhk", decode_rows, flat_keys, preferred_element_type=jnp.float32)
        * scaling
    )
    start_state = (
        jnp.full((steps * row_dev, heads_all), -jnp.inf, jnp.float32),
        jnp.zeros((steps * row_dev, heads_all), jnp.float32),
        jnp.zeros((steps * row_dev, heads_all, HEAD_DIM), jnp.float32),
    )
    partial_state = online_update(
        start_state, decode_scores, all_visible, flat_values, "rhk,kd->rhd"
    )
    merged = combined_all(partial_state, ("blk", "head"), merge_parts)
    merged = (
        merged[0].reshape(steps, row_dev, heads_all),
        merged[1].reshape(steps, row_dev, heads_all),
        merged[2].reshape(steps, row_dev, heads_all, HEAD_DIM),
    )
    step_rows = decode_queries.reshape(steps, row_dev, heads_all, HEAD_DIM)
    own_scores = (
        jnp.einsum("srhd,trd->srht", step_rows, new_keys, preferred_element_type=jnp.float32)
        * scaling
    )
    step_ids = jnp.arange(steps, dtype=jnp.int32)
    own_visible = (step_ids[None, :] <= step_ids[:, None])[:, None, None, :]
    final_decode = online_update(merged, own_scores, own_visible, new_values, "srht,trd->srhd")
    decode_out = (
        (final_decode[2] / final_decode[1][..., None])
        .astype(jnp.bfloat16)
        .reshape(steps, row_dev, decode_width)
    )
    return (prefill_out, decode_out)


def solution(mesh):
    placed = (
        P("groups", ("blk", "rep"), "head"),
        P("groups", ("blk", "head"), None),
        P("groups", ("blk", "head"), None),
        P("groups", ("blk", "head"), None),
        P("groups", ("blk", "head"), None),
        P("groups"),
        P("groups", "rep", None),
        P("groups", "rep", None),
        P("groups", "rep", None),
        P(("groups", "rep")),
    )
    return jax.shard_map(
        local,
        mesh=mesh,
        in_specs=placed,
        out_specs=(P("groups", ("blk", "rep"), "head"), P("groups", "rep", None)),
        check_vma=False,
    )
```

profile of v0, /device:TPU:0, one launch (start us, length us, event | category | flops | bytes accessed | tf_op | source)
XLA Modules:
  0.0 507.4 jit_solution(10840130970746726900)
XLA Ops:
  8.4 15.5 %all_to_all.105 = bf16[2,1536,128]{2,1,0:T(8,128)(2,1)} all-to-all(bf16[2,1536,128]{2,1,0:T(8,128)(2,1)S(1)} %pad_maximum_fusion), channel_id=1, replica_groups=mesh['groups'=2,'blk'=4,'head'=2,'rep'=2] {'head'}, dimensions={0} | all-to-all | bytes 1572864 | tf_op jit(solution)/shard_map/all_to_all | solution.py:136
  25.2 13.7 %all_to_all.106 = bf16[2,1536,128]{2,1,0:T(8,128)(2,1)} all-to-all(bf16[2,1536,128]{2,1,0:T(8,128)(2,1)S(1)} %pad_maximum_fusion.1), channel_id=1, replica_groups=mesh['groups'=2,'blk'=4,'head'=2,'rep'=2] {'head'}, dimensions={0} | all-to-all | bytes 1572864 | tf_op jit(solution)/shard_map/all_to_all | solution.py:137
  38.9 3.5 all-to-all-start.5
  43.0 4.5 all-to-all-done.5
  47.5 3.4 all-to-all-start.7
  53.0 3.1 all-to-all-done.7
  56.1 3.5 all-to-all-start.4
  61.5 4.7 all-to-all-done.4
  66.2 3.5 all-to-all-start.6
  69.7 6.3 %fusion.45 = (f32[128,8]{0,1:T(8,128)S(1)}, f32[3072,128,8]{1,0,2:T(8,128)}) fusion(pred[128,3072]{0,1:T(8,128)(4,1)S(1)} %copy.119, bf16[128,8,128]{2,1,0:T(8,128)(2,1)S(1)} %bitcast.208, bf16[1,1024,128]{2,1,0:T(8,128)(2,1)S(1)} %bitcast.206, bf16[1,2048,128]{2,1,0:T(8,128)(2,1)S(1)} %bitcast.203), kind=kOutput, calls=%fused_computation.68 | convolution fusion | flops 816315392 | bytes 14028800 | tf_op jit(solution)/shard_map/rhd,kd->rhk/dot_general | solution.py:184
  76.6 9.0 %fusion.53 = f32[128,8,128]{2,0,1:T(8,128)} fusion(f32[3072,128,8]{1,0,2:T(8,128)} %get-tuple-element.1117, f32[128,8]{0,1:T(8,128)S(1)} %get-tuple-element.1115, pred[128,3072]{0,1:T(8,128)(4,1)S(1)} %copy.119, bf16[1,1024,128]{2,1,0:T(8,128)(2,1)S(1)} %bitcast.207, bf16[1,2048,128]{2,1,0:T(8,128)(2,1)S(1)} %bitcast.204, f32[128,8]{0,1:T(8,128)S(1)} %get-tuple-element.1114), kind=kOutput, calls=%fused_computation.77 | convolution fusion | flops 822738944 | bytes 14295040 | tf_op jit(solution)/shard_map/rhk,kd->rhd/dot_general | solution.py:25
  87.0 3.6 all-to-all-start.1
  90.6 2.0 fusion.88
  93.3 7.6 %fusion.47 = f32[128,8]{0,1:T(8,128)} fusion(f32[3072,128,8]{1,0,2:T(8,128)} %get-tuple-element.1117, f32[128,8]{0,1:T(8,128)S(1)} %get-tuple-element.1115, pred[128,3072]{0,1:T(8,128)(4,1)S(1)} %copy.119), kind=kLoop, calls=%fused_computation.70 | loop fusion | flops 15727616 | bytes 12984320 | tf_op jit(solution)/shard_map/reduce_sum | solution.py:24
  102.1 49.7 %all-gather.8.cloned.1.call-done = bf16[1,12288,128]{2,1,0:T(8,128)(2,1)} async-done(((bf16[1,3072,128]{2,1,0:T(8,128)(2,1)}), bf16[1,12288,128]{2,1,0:T(8,128)(2,1)}) %all-gather.8.cloned.1.call-update) | async-done | bytes 3145744 | tf_op jit(solution)/shard_map/all_gather | solution.py:145
  153.3 238.3 %while.34 = (s32[]{:T(128)}, f32[1,512,8]{1,2,0:T(8,128)S(1)}, f32[1,512,8]{1,2,0:T(8,128)S(1)}, f32[1,512,8,128]{3,1,2,0:T(8,128)}, s32[2]{0:T(128)S(1)}, /*ind...) while((s32[]{:T(128)}, f32[1,512,8]{1,2,0:T(8,128)S(1)}, ...), condition=%wide.region_6.7_spmd.clone.clone, body=%wide.region_1.6_spmd.clone.clone.sunk | while | flops 13222868992 | bytes 324021760 | solution.py:90
  156.0 116.9 %conditional.4 = ((f32[1,512,8]{1,2,0:T(8,128)S(1)}, f32[1,512,8]{1,2,0:T(8,128)S(1)}, f32[1,512,8,128]{3,1,2,0:T(8,128)})) conditional(s32[]{:T(128)} %convert_element_type.48, (f32[1,512,8]{1,2,0:T(8,128)S(1)}, f32[1,512,8]{1,2,0:T(8,128)S(1)}, f32[1,512,8,128]{3,1,2,0:T(8,128)}) %tuple.262, (s32[6144]{0:T(1024)S(1)}, s32[]{:T(128)}, ...), branch_computations={%region_2.2_spmd, %region_3.5_spmd.clone} | conditional | flops 13222825984 | bytes 323871808 | solution.py:88
  157.9 5.7 %and_or_fusion = pred[512,6144]{0,1:T(8,128)(4,1)S(1)} fusion(s32[512]{0:T(512)S(1)} %broadcast_add_fusion, s32[6144]{0:T(1024)S(1)} %bitcast.198, pred[6144]{0:T(1024)(128)(4,1)S(1)} %fusion.34, pred[6144]{0:T(1024)(128)(4,1)S(1)} %fusion.32), kind=kLoop, calls=%fused_computation.25 | loop fusion | flops 9437184 | bytes 3184640 | tf_op jit(solution)/shard_map/while/body/eval_jaxpr/or | solution.py:73
  163.6 37.4 %fusion.18 = (f32[512,8]{0,1:T(8,128)S(1)}, f32[6144,512,8]{1,0,2:T(8,128)}) fusion(pred[512,6144]{0,1:T(8,128)(4,1)S(1)} %and_or_fusion, bf16[1,512,8,128]{3,1,2,0:T(8,128)(2,1)} %get-tuple-element.1017, bf16[2,1,6144,128]{3,2,1,0:T(8,128)(2,1)} %get-tuple-element.1015, s32[]{:T(128)} %get-tuple-element.1016), kind=kOutput, calls=%fused_computation.20 | convolution fusion | flops 6517944320 | bytes 106447360 | tf_op jit(solution)/shard_map/while/body/eval_jaxpr/cond/branch_1_fun/pqhd,pkd->pqhk/dot_general | solution.py:78
  201.0 31.6 %fusion.20 = f32[512,8]{0,1:T(8,128)S(1)} fusion(f32[6144,512,8]{1,0,2:T(8,128)} %get-tuple-element.1109, f32[512,8]{0,1:T(8,128)S(1)} %fusion.35, pred[512,6144]{0,1:T(8,128)(4,1)S(1)} %and_or_fusion), kind=kLoop, calls=%fused_computation.22 | loop fusion | flops 125825024 | bytes 103841792 | tf_op jit(solution)/shard_map/while/body/eval_jaxpr/cond/branch_1_fun/reduce_sum | solution.py:24
  232.7 40.3 %bitcast_add_fusion = f32[1,512,8,128]{3,1,2,0:T(8,128)} fusion(f32[1,512,8,128]{3,1,2,0:T(8,128)} %get-tuple-element.1019, f32[6144,512,8]{1,0,2:T(8,128)} %get-tuple-element.1109, f32[512,8]{0,1:T(8,128)S(1)} %fusion.35, pred[512,6144]{0,1:T(8,128)(4,1)S(1)} %and_or_fusion, bf16[2,1,6144,128]{3,2,1,0:T(8,128)(2,1)} %get-tuple-element.1020, ...), kind=kOutput, calls=%fused_computation.26 | convolution fusion | flops 6569328640 | bytes 109609472 | tf_op jit(solution)/shard_map/while/body/eval_jaxpr/cond/branch_1_fun/pqhk,pkd->pqhd/dot_general | solution.py:25
  275.5 115.9 %conditional.4 = ((f32[1,512,8]{1,2,0:T(8,128)S(1)}, f32[1,512,8]{1,2,0:T(8,128)S(1)}, f32[1,512,8,128]{3,1,2,0:T(8,128)})) conditional(s32[]{:T(128)} %convert_element_type.48, (f32[1,512,8]{1,2,0:T(8,128)S(1)}, f32[1,512,8]{1,2,0:T(8,128)S(1)}, f32[1,512,8,128]{3,1,2,0:T(8,128)}) %tuple.262, (s32[6144]{0:T(1024)S(1)}, s32[]{:T(128)}, ...), branch_computations={%region_2.2_spmd, %region_3.5_spmd.clone} | conditional | flops 13222825984 | bytes 323871808 | solution.py:88
  277.4 5.7 %and_or_fusion = pred[512,6144]{0,1:T(8,128)(4,1)S(1)} fusion(s32[512]{0:T(512)S(1)} %broadcast_add_fusion, s32[6144]{0:T(1024)S(1)} %bitcast.198, pred[6144]{0:T(1024)(128)(4,1)S(1)} %fusion.34, pred[6144]{0:T(1024)(128)(4,1)S(1)} %fusion.32), kind=kLoop, calls=%fused_computation.25 | loop fusion | flops 9437184 | bytes 3184640 | tf_op jit(solution)/shard_map/while/body/eval_jaxpr/or | solution.py:73
  283.1 36.6 %fusion.18 = (f32[512,8]{0,1:T(8,128)S(1)}, f32[6144,512,8]{1,0,2:T(8,128)}) fusion(pred[512,6144]{0,1:T(8,128)(4,1)S(1)} %and_or_fusion, bf16[1,512,8,128]{3,1,2,0:T(8,128)(2,1)} %get-tuple-element.1017, bf16[2,1,6144,128]{3,2,1,0:T(8,128)(2,1)} %get-tuple-element.1015, s32[]{:T(128)} %get-tuple-element.1016), kind=kOutput, calls=%fused_computation.20 | convolution fusion | flops 6517944320 | bytes 106447360 | tf_op jit(solution)/shard_map/while/body/eval_jaxpr/cond/branch_1_fun/pqhd,pkd->pqhk/dot_general | solution.py:78
  319.7 31.4 %fusion.20 = f32[512,8]{0,1:T(8,128)S(1)} fusion(f32[6144,512,8]{1,0,2:T(8,128)} %get-tuple-element.1109, f32[512,8]{0,1:T(8,128)S(1)} %fusion.35, pred[512,6144]{0,1:T(8,128)(4,1)S(1)} %and_or_fusion), kind=kLoop, calls=%fused_computation.22 | loop fusion | flops 125825024 | bytes 103841792 | tf_op jit(solution)/shard_map/while/body/eval_jaxpr/cond/branch_1_fun/reduce_sum | solution.py:24
  351.1 40.3 %bitcast_add_fusion = f32[1,512,8,128]{3,1,2,0:T(8,128)} fusion(f32[1,512,8,128]{3,1,2,0:T(8,128)} %get-tuple-element.1019, f32[6144,512,8]{1,0,2:T(8,128)} %get-tuple-element.1109, f32[512,8]{0,1:T(8,128)S(1)} %fusion.35, pred[512,6144]{0,1:T(8,128)(4,1)S(1)} %and_or_fusion, bf16[2,1,6144,128]{3,2,1,0:T(8,128)(2,1)} %get-tuple-element.1020, ...), kind=kOutput, calls=%fused_computation.26 | convolution fusion | flops 6569328640 | bytes 109609472 | tf_op jit(solution)/shard_map/while/body/eval_jaxpr/cond/branch_1_fun/pqhk,pkd->pqhd/dot_general | solution.py:25
  396.0 7.0 %reduce.20 = bf16[1024,512]{1,0:T(8,128)(2,1)S(1)} reduce(bf16[1024,1,512]{2,1,0:T(2,128)(2,1)S(1)} %bitcast.192, bf16[]{:T(256)} %broadcast.497), dimensions={1}, to_apply=%bitcast.174.reduce_sub_computation | reduce | bytes 2097154
  404.7 3.6 all-to-all-start.3
  408.3 37.5 %all-gather = f32[1024,8]{0,1:T(8,128)S(1)} all-gather(f32[128,8]{0,1:T(8,128)S(1)} %copy-done.5), channel_id=2, replica_groups=mesh['groups'=2,'blk'=4,'head'=2,'rep'=2] {'blk','head'}, dimensions={0}, use_global_device_ids=true | all-gather | bytes 36864 | tf_op jit(solution)/shard_map/all_gather | solution.py:10
  445.8 30.6 %all_gather.26 = f32[8,128,8]{1,2,0:T(8,128)S(1)} all-gather(f32[1,128,8]{1,2,0:T(8,128)S(1)} %fusion.79), channel_id=1, replica_groups=mesh['groups'=2,'blk'=4,'head'=2,'rep'=2] {'blk','head'}, dimensions={0}, use_global_device_ids=true | all-gather | bytes 36864 | tf_op jit(solution)/shard_map/all_gather | solution.py:10
  480.7 4.1 slice.33
  484.8 13.3 %while.33 = (s32[]{:T(128)}, f32[128,8]{0,1:T(8,128)S(1)}, f32[128,8]{0,1:T(8,128)S(1)}, f32[128,8,128]{2,1,0:T(8,128)S(1)}, f32[7,128,8]{1,2,0:T(8,128)S(1)}, /...) while((s32[]{:T(128)}, f32[128,8]{0,1:T(8,128)S(1)}, f32[128,8]{0,1:T(8,128)S(1)}, ...), condition=%wide.region_10.11_spmd, body=%wide.region_9.10_spmd.sunk | while | flops 401410 | bytes 2678885 | solution.py:13
  (149 shorter events, 42.0 us)
Async XLA Ops:
  7.2 491.8 %copy-start = (bf16[4,32,128]{2,1,0:T(8,128)(2,1)S(1)}, bf16[4,32,128]{2,1,0:T(8,128)(2,1)}, u32[]{:S(2)}) copy-start(bf16[4,32,128]{2,1,0:T(8,128)(2,1)} %param.24) | copy-start | bytes 98308
  7.2 94.9 %all-gather.6.cloned.1.call-start = ((), (), s32[]{:S(2)}) async-start(), calls=%async_computation.8 | async-start | bytes 3932160 | tf_op jit(solution)/shard_map/all_gather | solution.py:144
  23.9 127.8 %all-gather.8.cloned.1.call-start = ((), (), s32[]{:S(2)}) async-start(), calls=%async_computation.9 | async-start | bytes 3932160 | tf_op jit(solution)/shard_map/all_gather | solution.py:145
  38.9 8.6 %all-to-all-start.5 = ((bf16[2,512,128]{2,1,0:T(8,128)(2,1)}), bf16[2,512,128]{2,1,0:T(8,128)(2,1)S(1)}, u32[]{:S(2)}, u32[]{:S(2)}) async-start(bf16[2,512,128]{2,1,0:T(8,128)(2,1)} %param.19), calls=%async_computation.5 | async-start | bytes 524288 | tf_op jit(solution)/shard_map/all_to_all | solution.py:160
  47.5 8.6 %all-to-all-start.7 = ((bf16[2,512,128]{2,1,0:T(8,128)(2,1)}), bf16[2,512,128]{2,1,0:T(8,128)(2,1)S(1)}, u32[]{:S(2)}, u32[]{:S(2)}) async-start(bf16[2,512,128]{2,1,0:T(8,128)(2,1)} %param.20), calls=%async_computation.7 | async-start | bytes 524288 | tf_op jit(solution)/shard_map/all_to_all | solution.py:161
  56.1 10.1 %all-to-all-start.4 = ((bf16[2,1024,128]{2,1,0:T(8,128)(2,1)}), bf16[2,1024,128]{2,1,0:T(8,128)(2,1)S(1)}, u32[]{:S(2)}, u32[]{:S(2)}) async-start(bf16[2,1024,128]{2,1,0:T(8,128)(2,1)} %param.17), calls=%async_computation.4 | async-start | bytes 1048576 | tf_op jit(solution)/shard_map/all_to_all | solution.py:158
  66.2 10.1 %all-to-all-start.6 = ((bf16[2,1024,128]{2,1,0:T(8,128)(2,1)}), bf16[2,1024,128]{2,1,0:T(8,128)(2,1)S(1)}, u32[]{:S(2)}, u32[]{:S(2)}) async-start(bf16[2,1024,128]{2,1,0:T(8,128)(2,1)} %param.18), calls=%async_computation.6 | async-start | bytes 1048576 | tf_op jit(solution)/shard_map/all_to_all | solution.py:159
  69.7 409.6 %all-gather.10.cloned.1.call-start = ((), (), s32[]{:S(2)}) async-start(), calls=%async_computation.10 | async-start | bytes 4718592 | tf_op jit(solution)/shard_map/all_gather | solution.py:10
  76.0 0.6 copy-start.4
  76.6 9.0 %copy-start.1 = (bf16[2,512,512]{2,1,0:T(8,128)(2,1)S(1)}, bf16[2,512,512]{2,1,0:T(8,128)(2,1)}, u32[]{:S(2)}) copy-start(bf16[2,512,512]{2,1,0:T(8,128)(2,1)} %param.16) | copy-start | bytes 3145732
  76.6 14.0 %copy-start.9 = (bf16[4,32,128]{2,1,0:T(8,128)(2,1)S(1)}, bf16[4,32,128]{2,1,0:T(8,128)(2,1)}, u32[]{:S(2)}) copy-start(bf16[4,32,128]{2,1,0:T(8,128)(2,1)} %param.23) | copy-start | bytes 98308
  87.0 13.9 %all-to-all-start.1 = ((bf16[2,512,512]{1,2,0:T(8,128)(2,1)}), bf16[2,512,512]{1,2,0:T(8,128)(2,1)S(1)}, u32[]{:S(2)}, u32[]{:S(2)}) async-start(bf16[2,512,512]{1,2,0:T(8,128)(2,1)} %copy.115), calls=%async_computation.1 | async-start | bytes 2097152 | tf_op jit(solution)/shard_map/all_to_all | solution.py:128
  90.6 62.7 %copy-start.7 = (pred[4,4]{1,0:T(4,128)(4,1)}, pred[4,4]{1,0:T(4,128)(4,1)S(1)}, u32[]{:S(2)}) copy-start(pred[4,4]{1,0:T(4,128)(4,1)S(1)} %iota_compare_fusion.1) | copy-start | bytes 52
  391.6 16.6 %copy-start.5 = (f32[128,8]{0,1:T(8,128)S(1)}, f32[128,8]{0,1:T(8,128)}, u32[]{:S(2)}) copy-start(f32[128,8]{0,1:T(8,128)} %copy-done.4) | copy-start | bytes 12292
  391.6 16.6 %copy-start.6 = (f32[128,8]{0,1:T(8,128)S(1)}, f32[128,8]{0,1:T(8,128)}, u32[]{:S(2)}) copy-start(f32[128,8]{0,1:T(8,128)} %fusion.47) | copy-start | bytes 12292
  404.7 71.7 %all-to-all-start.3 = ((bf16[2,2,131072]{2,1,0:T(2,128)(2,1)}), bf16[2,2,131072]{2,1,0:T(2,128)(2,1)S(1)}, u32[]{:S(2)}, u32[]{:S(2)}) async-start(bf16[2,2,131072]{2,1,0:T(2,128)(2,1)} %reshape.538), calls=%async_computation.3 | async-start | bytes 2097152 | tf_op jit(solution)/shard_map/all_to_all | solution.py:154
  479.2 19.0 %copy-start.3 = (f32[4,32,8]{1,2,0:T(8,128)S(1)}, f32[4,32,8]{1,2,0:T(8,128)}, u32[]{:S(2)}) copy-start(f32[4,32,8]{1,2,0:T(8,128)} %copy.127) | copy-start | bytes 12292
  479.2 19.1 %copy-start.2 = (f32[4,32,8,4]{2,3,0,1:T(4,128)S(1)}, f32[4,32,8,4]{2,3,0,1:T(4,128)}, u32[]{:S(2)}) copy-start(f32[4,32,8,4]{2,3,0,1:T(4,128)} %get-tuple-element.1119) | copy-start | bytes 49156
  479.2 19.1 %copy-start.8 = (pred[4,4]{1,0:T(4,128)(4,1)S(1)}, pred[4,4]{1,0:T(4,128)(4,1)}, u32[]{:S(2)}) copy-start(pred[4,4]{1,0:T(4,128)(4,1)} %copy-done.7) | copy-start | bytes 52
Sparse Core Ops, SparseCore 0:
  24.1 63.9 all-gather.5
  89.7 62.0 all-gather.7
  154.0 71.4 all-gather.9
where the time goes:
time: 516 us; the launch traced here: 507 us
  matrix products  172 us (33%)
  other arithmetic  102 us (20%)
  blocking collectives  97.3 us (19%)
  waiting for transfers between devices  62.2 us (12%)
  local copies, waits for them, and re-layouts  32.6 us (6%)
  starting transfers between devices  21.2 us (4%)
  between operations  14.5 us (3%)
  loops' own time  5.61 us (1%)
    dot_general x4, matrix products, online_update(): jnp.einsum(einsum_form, weights.astype(jnp.bfloat16), values_block, prefe...  90.1 us
    dot_general x2, matrix products, update(): jnp.einsum('pqhd,pkd->pqhk', query_block, keys_now, preferred_element_typ...  74 us
    reduce_sum x4, other arithmetic, online_update(): totals = totals * factor + jnp.sum(weights, axis=-1)  70.9 us
    all_gather x2, blocking collectives, combined_all(): pieces = jax.tree.map(lambda part: lax.all_gather(part, axis), value)  68.1 us
    all_gather x1, waiting for transfers between devices, local(): lax.all_gather(mine_values, 'blk', axis=1, tiled=True)  49.7 us
    all_to_all x1, blocking collectives, local(): lax.all_to_all(local_keys, 'head', split_axis=0, concat_axis=1, tiled=True)  15.5 us
    all_to_all x1, blocking collectives, local(): lax.all_to_all(local_values, 'head', split_axis=0, concat_axis=1, tiled=T...  13.7 us
    or x2, other arithmetic, advance(): visible = prefix_ok[:, None, None, :] | stretch_ok[None, :, None, :]  11.4 us
  transfers between devices with their start and end apart: 9, of which 5 were waited for; matrix products, arithmetic and copies ran while one was open for 56% of the time, Pallas kernels for 0%

commit v1 on v0

v1 whole, which is shorter than its diff:
```python
import functools

import jax
import jax.numpy as jnp
from jax import lax
from jax.experimental import pallas as pl
from jax.experimental.pallas import tpu as pltpu
from jax.sharding import PartitionSpec as P

HEAD_DIM = 128
SCALE_LOG2E = HEAD_DIM ** (-0.5) * 1.4426950408889634
LOW = -1e30


def fold(q, k, v, m_ref, acc_ref, bias=None):
    s = lax.dot_general(q, k, (((1,), (1,)), ((), ())), preferred_element_type=jnp.float32)
    if bias is not None:
        s = jnp.where(bias, s, LOW)
    m_prev = m_ref[...]
    m_new = jnp.maximum(m_prev, jnp.max(s, axis=-1, keepdims=True))
    p = jnp.exp2(s * SCALE_LOG2E - (m_new * SCALE_LOG2E)[:, :1]).astype(jnp.bfloat16)
    alpha = jnp.exp2((m_prev - m_new) * SCALE_LOG2E)
    alpha2 = jnp.concatenate([alpha, alpha], axis=1)
    pv = jnp.dot(p, v, preferred_element_type=jnp.float32)
    acc_ref[...] = acc_ref[...] * alpha2 + pv
    m_ref[...] = m_new


def start_state(m_ref, acc_ref):
    m_ref[...] = jnp.full_like(m_ref, LOW)
    acc_ref[...] = jnp.zeros_like(acc_ref)


def fold_prefix(q, k_ref, v2_ref, length, block, m_ref, acc_ref):
    full = length // block

    @pl.loop(0, full)
    def _(i):
        rows = pl.ds(pl.multiple_of(i * block, block), block)
        fold(q, k_ref[rows, :], v2_ref[rows, :], m_ref, acc_ref)

    @pl.when(full * block < length)
    def _():
        rows = pl.ds(pl.multiple_of(full * block, block), block)
        spot = full * block + lax.broadcasted_iota(jnp.int32, (q.shape[0], block), 1)
        fold(q, k_ref[rows, :], v2_ref[rows, :], m_ref, acc_ref, spot < length)


def finish(acc_ref):
    return (acc_ref[:, :HEAD_DIM] / acc_ref[:, HEAD_DIM:]).astype(jnp.bfloat16)


def prefill_kernel(block, info, q_ref, pre_ref, chk_ref, o_ref, pv2, cv2, m_ref, acc_ref):
    q_rows = q_ref.shape[1]

    @pl.when(pl.program_id(0) == 0)
    def _():
        pv2[:, :HEAD_DIM] = pre_ref[1]
        pv2[:, HEAD_DIM:] = jnp.ones((pv2.shape[0], HEAD_DIM), jnp.bfloat16)
        cv2[:, :HEAD_DIM] = chk_ref[1]
        cv2[:, HEAD_DIM:] = jnp.ones((cv2.shape[0], HEAD_DIM), jnp.bfloat16)

    q = q_ref[0]
    start_state(m_ref, acc_ref)
    here = info[1]
    rows = pl.ds(pl.multiple_of(here * q_rows, q_rows), q_rows)
    seen = lax.broadcasted_iota(jnp.int32, (q_rows, q_rows), 1) <= lax.broadcasted_iota(
        jnp.int32, (q_rows, q_rows), 0
    )
    fold(q, chk_ref[0, rows, :], cv2[rows, :], m_ref, acc_ref, seen)

    @pl.loop(0, here)
    def _(i):
        rows = pl.ds(pl.multiple_of(i * q_rows, q_rows), q_rows)
        fold(q, chk_ref[0, rows, :], cv2[rows, :], m_ref, acc_ref)

    fold_prefix(q, pre_ref.at[0], pv2, info[0], block, m_ref, acc_ref)
    o_ref[0] = finish(acc_ref)


def decode_kernel(
    block, heads, row_dev, info, q_ref, nk_ref, nv_ref, pre_ref, chk_ref, o_ref, pv2, cv2, nv2, m_ref, acc_ref
):
    pv2[:, :HEAD_DIM] = pre_ref[1]
    pv2[:, HEAD_DIM:] = jnp.ones((pv2.shape[0], HEAD_DIM), jnp.bfloat16)
    cv2[:, :HEAD_DIM] = chk_ref[1]
    cv2[:, HEAD_DIM:] = jnp.ones((cv2.shape[0], HEAD_DIM), jnp.bfloat16)
    nv2[:, :HEAD_DIM] = nv_ref[...]
    nv2[:, HEAD_DIM:] = jnp.ones((nv2.shape[0], HEAD_DIM), jnp.bfloat16)
    q = q_ref[...]
    start_state(m_ref, acc_ref)
    count = q.shape[0]
    fresh = nk_ref.shape[0]
    row = info[1] * count + lax.broadcasted_iota(jnp.int32, (count, fresh), 0)
    col = lax.broadcasted_iota(jnp.int32, (count, fresh), 1)
    own = ((row // heads) % row_dev == col % row_dev) & (col // row_dev <= row // (heads * row_dev))
    fold(q, nk_ref[...], nv2[...], m_ref, acc_ref, own)

    @pl.loop(0, chk_ref.shape[1] // block)
    def _(i):
        rows = pl.ds(pl.multiple_of(i * block, block), block)
        fold(q, chk_ref[0, rows, :], cv2[rows, :], m_ref, acc_ref)

    fold_prefix(q, pre_ref.at[0], pv2, info[0], block, m_ref, acc_ref)
    o_ref[...] = finish(acc_ref)


def prefill(info, q, pre, chk, block):
    _, q_rows, width = q.shape
    heads = width // HEAD_DIM
    return pl.pallas_call(
        functools.partial(prefill_kernel, block),
        out_shape=jax.ShapeDtypeStruct(q.shape, jnp.bfloat16),
        grid_spec=pltpu.PrefetchScalarGridSpec(
            num_scalar_prefetch=1,
            grid=(heads,),
            in_specs=[
                pl.BlockSpec((1, q_rows, HEAD_DIM), lambda h, info: (0, 0, h)),
                pl.BlockSpec(pre.shape, lambda h, info: (0, 0, 0), pipeline_mode=pl.Buffered(1)),
                pl.BlockSpec(chk.shape, lambda h, info: (0, 0, 0), pipeline_mode=pl.Buffered(1)),
            ],
            out_specs=pl.BlockSpec((1, q_rows, HEAD_DIM), lambda h, info: (0, 0, h)),
            scratch_shapes=[
                pltpu.VMEM((pre.shape[1], 2 * HEAD_DIM), jnp.bfloat16),
                pltpu.VMEM((chk.shape[1], 2 * HEAD_DIM), jnp.bfloat16),
                pltpu.VMEM((q_rows, HEAD_DIM), jnp.float32),
                pltpu.VMEM((q_rows, 2 * HEAD_DIM), jnp.float32),
            ],
        ),
        compiler_params=pltpu.CompilerParams(
            dimension_semantics=("arbitrary",), vmem_limit_bytes=56 * 2**20
        ),
        name="prefill",
    )(info, q, pre, chk)


def decode(info, q, nk, nv, pre, chk, block, heads, row_dev):
    whole = pl.BlockSpec(memory_space=pltpu.VMEM)
    return pl.pallas_call(
        functools.partial(decode_kernel, block, heads, row_dev),
        out_shape=jax.ShapeDtypeStruct(q.shape, jnp.bfloat16),
        in_specs=[pl.BlockSpec(memory_space=pltpu.SMEM)] + [whole] * 5,
        out_specs=whole,
        scratch_shapes=[
            pltpu.VMEM((pre.shape[1], 2 * HEAD_DIM), jnp.bfloat16),
            pltpu.VMEM((chk.shape[1], 2 * HEAD_DIM), jnp.bfloat16),
            pltpu.VMEM((nk.shape[0], 2 * HEAD_DIM), jnp.bfloat16),
            pltpu.VMEM((q.shape[0], HEAD_DIM), jnp.float32),
            pltpu.VMEM((q.shape[0], 2 * HEAD_DIM), jnp.float32),
        ],
        compiler_params=pltpu.CompilerParams(vmem_limit_bytes=56 * 2**20),
        name="decode",
    )(info, q, nk, nv, pre, chk)


def local(
    queries,
    prefix_keys,
    prefix_values,
    stretch_keys,
    stretch_values,
    prefix_lengths,
    decode_queries,
    new_keys,
    new_values,
    row_prompts,
):
    prompts, q_rows, width = queries.shape
    heads_axis, blk_axis = lax.axis_size("head"), lax.axis_size("blk")
    assert prompts == heads_axis and lax.axis_size("rep") == 2
    side = lax.axis_index("rep") == 0
    pre = jnp.where(side, prefix_keys, prefix_values)
    chk = jnp.where(side, stretch_keys, stretch_values)
    pre_rows = pre.shape[1]
    both = jnp.concatenate([pre, chk], axis=1)
    moved = lax.all_to_all(both, "head", split_axis=0, concat_axis=0, tiled=True)
    gathered = lax.all_gather(moved, "blk", axis=0, tiled=True)
    gathered = lax.all_gather(gathered, "rep", axis=0)
    pre_all = gathered[:, :, :pre_rows].reshape(2, -1, HEAD_DIM)
    chk_all = gathered[:, :, pre_rows:].reshape(2, -1, HEAD_DIM)
    mine = lax.all_to_all(queries, "head", split_axis=0, concat_axis=2, tiled=True)
    length = lax.dynamic_index_in_dim(prefix_lengths, lax.axis_index("head"), keepdims=False)
    block = 1024

    steps, row_dev, decode_width = decode_queries.shape
    heads_all = decode_width // HEAD_DIM
    rows_all = steps * row_dev * heads_all
    share = rows_all // blk_axis
    dq = lax.dynamic_slice_in_dim(
        decode_queries.reshape(rows_all, HEAD_DIM), lax.axis_index("blk") * share, share, 0
    )
    dec = decode(
        jnp.stack([length, lax.axis_index("blk")]).astype(jnp.int32),
        dq,
        new_keys.reshape(-1, HEAD_DIM),
        new_values.reshape(-1, HEAD_DIM),
        pre_all,
        chk_all,
        block,
        heads_all,
        row_dev,
    )
    dec_all = lax.all_gather(dec, ("head", "blk"), axis=0, tiled=True)
    dec_all = dec_all.reshape(heads_axis, steps, row_dev, decode_width)
    decode_out = dec_all[0]
    for index in range(1, heads_axis):
        decode_out = jnp.where((row_prompts == index)[None, :, None], dec_all[index], decode_out)

    out = prefill(
        jnp.stack([length, lax.axis_index(("blk", "rep"))]).astype(jnp.int32), mine, pre_all, chk_all, block
    )
    prefill_out = lax.all_to_all(out, "head", split_axis=2, concat_axis=0, tiled=True)
    return (prefill_out, decode_out)


def solution(mesh):
    placed = (
        P("groups", ("blk", "rep"), "head"),
        P("groups", ("blk", "head"), None),
        P("groups", ("blk", "head"), None),
        P("groups", ("blk", "head"), None),
        P("groups", ("blk", "head"), None),
        P("groups"),
        P("groups", "rep", None),
        P("groups", "rep", None),
        P("groups", "rep", None),
        P(("groups", "rep")),
    )
    return jax.shard_map(
        local,
        mesh=mesh,
        in_specs=placed,
        out_specs=(P("groups", ("blk", "rep"), "head"), P("groups", "rep", None)),
        check_vma=False,
    )
```

time: 516 us -> 363 us (0.70)
  matrix products: 172 us -> 0 us
  other arithmetic: 102 us -> 12.6 us
  Pallas kernels: 0 us -> 64.1 us
  starting transfers between devices: 21.2 us -> 70 us
  local copies, waits for them, and re-layouts: 32.6 us -> 20 us
  waiting for transfers between devices: 62.2 us -> 73.8 us
  blocking collectives: 97.3 us -> 105 us
  loops' own time: 5.61 us -> 0 us
    dot_general x8 -> x0, matrix products: 172 us -> none  [the longest x4 90.1 us: online_update(): jnp.einsum(einsum_form, weights.astype(jnp.bfloat16), values_block, prefe...]
    reduce_sum x5 -> x0, other arithmetic: 72.2 us -> none  [the longest x4 70.9 us: online_update(): totals = totals * factor + jnp.sum(weights, axis=-1)]
    pallas_call x0 -> x2, Pallas kernels: none -> 64.1 us  [the longest x1 52 us: prefill(): pl.pallas_call(functools.partial(prefill_kernel, block), out_shape=jax.Sh...]
    all_to_all x5 -> x1, starting transfers between devices: 17.5 us -> 66.2 us  [local(): lax.all_to_all(out, 'head', split_axis=2, concat_axis=0, tiled=True)]
    all_gather x2 -> x1, blocking collectives: 68.1 us -> 89.2 us  [local(): dec_all = lax.all_gather(dec, ('head', 'blk'), axis=0, tiled=True)]
    all_gather x3 -> x2, waiting for transfers between devices: 49.7 us -> 64.1 us  [the longest x1 64.1 us: local(): gathered = lax.all_gather(moved, 'blk', axis=0, tiled=True)]
    all_to_all x2 -> x1, blocking collectives: 29.2 us -> 15.5 us  [local(): lax.all_to_all(both, 'head', split_axis=0, concat_axis=0, tiled=True)]
    all_to_all x5 -> x1, waiting for transfers between devices: 12.5 us -> 0.01 us  [local(): lax.all_to_all(out, 'head', split_axis=2, concat_axis=0, tiled=True)]
  transfers between devices with their start and end apart: 9 -> 4, of which waited for: 5 -> 2; matrix products, arithmetic and copies ran while one was open for 56% -> 2% of each run, Pallas kernels for 0% -> 3%
where the time goes in v1:
time: 363 us; the launch traced here: 359 us
  blocking collectives  105 us (29%)
  waiting for transfers between devices  73.8 us (20%)
  starting transfers between devices  70 us (19%)
  Pallas kernels  64.1 us (18%)
  local copies, waits for them, and re-layouts  20 us (6%)
  between operations  14.2 us (4%)
  other arithmetic  12.6 us (3%)
    all_gather x1, blocking collectives, local(): dec_all = lax.all_gather(dec, ('head', 'blk'), axis=0, tiled=True)  89.2 us
    all_to_all x1, starting transfers between devices, local(): lax.all_to_all(out, 'head', split_axis=2, concat_axis=0, tiled=True)  66.2 us
    all_gather x1, waiting for transfers between devices, local(): gathered = lax.all_gather(moved, 'blk', axis=0, tiled=True)  64.1 us
    pallas_call x1, Pallas kernels, prefill(): pl.pallas_call(functools.partial(prefill_kernel, block), out_shape=jax.Sh...  52 us
    all_to_all x1, blocking collectives, local(): lax.all_to_all(both, 'head', split_axis=0, concat_axis=0, tiled=True)  15.5 us
    pallas_call x1, Pallas kernels, decode(): pl.pallas_call(functools.partial(decode_kernel, block, heads, row_dev), o...  12.1 us
    all_to_all x1, waiting for transfers between devices, local(): lax.all_to_all(queries, 'head', split_axis=0, concat_axis=2, tiled=True)  9.68 us
  transfers between devices with their start and end apart: 4, of which 2 were waited for; matrix products, arithmetic and copies ran while one was open for 2% of the time, Pallas kernels for 3%

profile of v1, /device:TPU:0, one launch (start us, length us, event | category | flops | bytes accessed | tf_op | source)
XLA Modules:
  0.0 359.3 jit_solution(204824519314016238)
XLA Ops:
  7.2 0.0 all-gather.4.cloned.1.call-start
  7.2 1.1 broadcast_select_fusion
  8.3 1.0 broadcast_select_fusion.2
  9.3 0.1 pad_maximum_fusion
  9.4 15.5 %all_to_all.41 = bf16[2,1536,128]{2,1,0:T(8,128)(2,1)} all-to-all(bf16[2,1536,128]{2,1,0:T(8,128)(2,1)S(1)} %pad_maximum_fusion), channel_id=1, replica_groups=mesh['groups'=2,'blk'=4,'head'=2,'rep'=2] {'head'}, dimensions={0} | all-to-all | bytes 1572864 | tf_op jit(solution)/shard_map/all_to_all | solution.py:176
  24.9 0.0 all-gather.4.cloned.1.call-update
  24.9 0.0 all-gather.6.cloned.1.call-start
  24.9 64.1 %all-gather.4.cloned.1.call-done = bf16[8,1536,128]{2,1,0:T(8,128)(2,1)} async-done(((bf16[2,1536,128]{2,1,0:T(8,128)(2,1)}), bf16[8,1536,128]{2,1,0:T(8,128)(2,1)}) %all-gather.4.cloned.1.call-update) | async-done | bytes 3145744 | tf_op jit(solution)/shard_map/all_gather | solution.py:177
  89.1 3.7 %all-to-all-start = ((bf16[2,512,512]{2,1,0:T(8,128)(2,1)}), bf16[2,512,512]{2,1,0:T(8,128)(2,1)S(1)}, u32[]{:S(2)}, u32[]{:S(2)}) async-start(bf16[2,512,512]{2,1,0:T(8,128)(2,1)} %param.10), calls=%async_computation | async-start | bytes 2097152 | tf_op jit(solution)/shard_map/all_to_all | solution.py:181
  92.8 0.1 reshape.27
  93.0 0.7 dynamic_slice.7
  93.6 1.3 pad_add_fusion.1.info
  94.9 1.3 pad_add_fusion.info
  96.2 0.6 constant_dynamic-slice_fusion.q_ref
  96.8 9.7 %all-to-all-done = bf16[2,512,512]{2,1,0:T(8,128)(2,1)S(1)} async-done(((bf16[2,512,512]{2,1,0:T(8,128)(2,1)}), bf16[2,512,512]{2,1,0:T(8,128)(2,1)S(1)}, u32[]{:S(2)}, u32[]{:S(2)}) %all-to-all-start) | async-done | bytes 1048608 | tf_op jit(solution)/shard_map/all_to_all | solution.py:181
  106.5 1.1 copy.21
  107.6 4.6 %slice.18 = bf16[2,8,1024,128]{3,2,1,0:T(8,128)(2,1)} slice(bf16[2,8,1536,128]{3,2,1,0:T(8,128)(2,1)} %bitcast.25), slice={[0:2], [0:8], [0:1024], [0:128]} | slice | bytes 8388608 | tf_op jit(solution)/shard_map/slice | solution.py:179
  112.3 3.1 slice.19
  115.4 52.0 %prefill.1 = bf16[1,512,1024]{2,1,0:T(8,128)(2,1)} custom-call(s32[2]{0:T(128)} %pad_add_fusion.info, bf16[1,512,1024]{2,1,0:T(8,128)(2,1)} %bitcast.27, bf16[2,8192,128]{2,1,0:T(8,128)(2,1)} %bitcast.19, bf16[2,4096,128]{2,1,0:T(8,128)(2,1)} %bitcast.21), custom_call_target="tpu_custom_call" | custom-call | tf_op jit(solution)/shard_map/prefill/pallas_call | solution.py:111
  167.4 4.8 %copy.18 = bf16[1,512,1024]{1,0,2:T(2,128)(2,1)S(1)} copy(bf16[1,512,1024]{2,1,0:T(8,128)(2,1)} %prefill.1) | data formatting | bytes 2097152 | tf_op jit(solution)/shard_map/prefill/pallas_call | solution.py:111
  172.2 0.5 broadcast.1
  172.7 7.0 %reduce = bf16[1024,512]{1,0:T(8,128)(2,1)S(1)} reduce(bf16[1024,1,512]{2,1,0:T(2,128)(2,1)S(1)} %bitcast.24, bf16[]{:T(256)} %broadcast.1), dimensions={1}, to_apply=%bitcast.17.reduce_sub_computation | reduce | bytes 2097154
  179.7 1.6 reshape.31
  181.3 66.2 %all-to-all-start.2 = ((bf16[2,2,131072]{2,1,0:T(2,128)(2,1)}), bf16[2,2,131072]{2,1,0:T(2,128)(2,1)S(1)}, u32[]{:S(2)}, u32[]{:S(2)}) async-start(bf16[2,2,131072]{2,1,0:T(2,128)(2,1)} %reshape.31), calls=%async_computation.2 | async-start | bytes 2097152 | tf_op jit(solution)/shard_map/all_to_all | solution.py:212
  247.6 12.1 %decode.1 = bf16[256,128]{1,0:T(8,128)(2,1)} custom-call(s32[2]{0:T(128)} %pad_add_fusion.1.info, bf16[256,128]{1,0:T(8,128)(2,1)} %constant_dynamic-slice_fusion.q_ref, bf16[128,128]{1,0:T(8,128)(2,1)} %bitcast.30, bf16[128,128]{1,0:T(8,128)(2,1)} %bitcast.31, bf16[2,8192,128]{2,1,0:T(8,128)(2,1)} %bitcast.20, bf16[2,4096,128]{2,1,0:T(8,128)(2,1)} %bitcast.22), custom_call_target="tpu_custom_call" | custom-call | tf_op jit(solution)/shard_map/decode/pallas_call | solution.py:139
  259.7 89.2 %all_gather.15 = bf16[2048,128]{1,0:T(8,128)(2,1)S(1)} all-gather(bf16[256,128]{1,0:T(8,128)(2,1)} %decode.1), channel_id=1, replica_groups=mesh['groups'=2,'blk'=4,'head'=2,'rep'=2] {'head','blk'}, dimensions={0}, use_global_device_ids=true | all-gather | bytes 589824 | tf_op jit(solution)/shard_map/all_gather | solution.py:203
  348.9 0.1 squeeze.8
  349.0 0.1 squeeze.9
  349.2 0.8 broadcast_select_fusion.1
  350.0 0.9 reshape.32
  350.9 0.3 copy.20
  351.2 1.3 copy.19
  (11 shorter events, 0.1 us)
Async XLA Ops:
  7.2 81.9 %all-gather.4.cloned.1.call-start = ((), (), s32[]{:S(2)}) async-start(), calls=%async_computation.3 | async-start | bytes 3932160 | tf_op jit(solution)/shard_map/all_gather | solution.py:177
  24.9 82.8 %all-gather.6.cloned.1.call-start = ((), (), s32[]{:S(2)}) async-start(), calls=%async_computation.4 | async-start | bytes 9437184 | tf_op jit(solution)/shard_map/all_gather | solution.py:178
  89.0 3.8 %copy-start = (bf16[4,32,1024]{2,1,0:T(8,128)(2,1)S(1)}, bf16[4,32,1024]{2,1,0:T(8,128)(2,1)}, u32[]{:S(2)}) copy-start(bf16[4,32,1024]{2,1,0:T(8,128)(2,1)} %param.16) | copy-start | bytes 786436
  89.1 3.9 %copy-start.1 = (s32[2]{0:T(128)S(1)}, s32[2]{0:T(128)}, u32[]{:S(2)}) copy-start(s32[2]{0:T(128)} %param.15) | copy-start | bytes 28
  89.1 7.7 %copy-start.2 = (s32[32]{0:T(128)S(1)}, s32[32]{0:T(128)}, u32[]{:S(2)}) copy-start(s32[32]{0:T(128)} %param.19) | copy-start | bytes 388
  89.1 17.4 %all-to-all-start = ((bf16[2,512,512]{2,1,0:T(8,128)(2,1)}), bf16[2,512,512]{2,1,0:T(8,128)(2,1)S(1)}, u32[]{:S(2)}, u32[]{:S(2)}) async-start(bf16[2,512,512]{2,1,0:T(8,128)(2,1)} %param.10), calls=%async_computation | async-start | bytes 2097152 | tf_op jit(solution)/shard_map/all_to_all | solution.py:181
  181.3 168.6 %all-to-all-start.2 = ((bf16[2,2,131072]{2,1,0:T(2,128)(2,1)}), bf16[2,2,131072]{2,1,0:T(2,128)(2,1)S(1)}, u32[]{:S(2)}, u32[]{:S(2)}) async-start(bf16[2,2,131072]{2,1,0:T(2,128)(2,1)} %reshape.31), calls=%async_computation.2 | async-start | bytes 2097152 | tf_op jit(solution)/shard_map/all_to_all | solution.py:212
Sparse Core Ops, SparseCore 0:
  25.0 63.9 all-gather.3
  90.6 15.3 all-gather.5
